TPU v7x, 512 devices: a whole 4x8x8 slice. The times are simulated.
512 devices in a mesh: row: 8 (over z_lo, x), col: 8 (over z_hi, core), panel: 8 (over y).
Axes of the slice: x: 4, y: 8, z: 8 (z_hi: 4, z_lo: 2; z = z_hi * 2 + z_lo), core: 2. Of those that a mesh axis runs over, the one named last changes fastest.
Arguments:
- velocity: bfloat16 [4608, 6, 4096], P(('row', 'col'), None, 'panel'), may hold values from -6 to 6
- panel_weight: float32 [4096], P('panel'), may hold values from -0.109375 to 0.109375
- panel_group: int32 [4096], P('panel'), may hold values from 0 to 3
- tile_map: int32 [8, 8], replicated, may hold values from 0 to 3
- group_gain: float32 [4, 4], replicated, may hold values from 0.25 to 1
Outputs:
- qtf: float32 [4608, 2, 4608], P(('row', 'panel'), None, 'col')
All inputs are finite; a program needn't handle non-finite values.
Results may differ from a plain program's by a relative error of at most 0.0029.
Values may be sent and summed in bfloat16 or wider, within the bound.
A program may use at most 64 MiB of HBM per device.

v0:
```python
import jax
import jax.numpy as jnp
from jax import lax
from jax.sharding import PartitionSpec as P


def spread(value, axis, source):
    kept = jnp.where(lax.axis_index(axis) == source, value, 0).astype(value.dtype)
    return lax.psum(kept, axis)


def contract(left_side, right_side):
    return lax.dot_general(
        left_side, right_side, (((1,), (1,)), ((), ())), preferred_element_type=jnp.float32
    )


def pair_products(row_piece, right_side, tile_sign, half_depth):
    left_re = row_piece[:, :half_depth]
    left_im = row_piece[:, half_depth:]
    right_re = right_side[:, :half_depth]
    right_im = right_side[:, half_depth:]
    real_part = contract(left_re, right_re) + tile_sign * contract(left_im, right_im)
    imag_part = contract(left_im, right_re) - tile_sign * contract(left_re, right_im)
    return jnp.stack((real_part, imag_part), axis=1)


def local(velocity, panel_weight, panel_group, tile_map, group_gain):
    row_index = lax.axis_index("row")
    col_index = lax.axis_index("col")
    rows_block = lax.all_gather(velocity, "col", axis=0, tiled=True)
    cols_block = spread(rows_block, "row", col_index)
    chosen = (lax.broadcasted_iota(jnp.int32, tile_map.shape, 0) == row_index) & (
        lax.broadcasted_iota(jnp.int32, tile_map.shape, 1) == col_index
    )
    region = jnp.sum(jnp.where(chosen, tile_map, 0))
    group_count = group_gain.shape[0]
    case_cols = lax.broadcasted_iota(jnp.int32, group_gain.shape, 1)
    case_gains = jnp.sum(jnp.where(case_cols == region, group_gain, jnp.float32(0.0)), axis=1)
    group_ids = lax.broadcasted_iota(jnp.int32, (panel_group.shape[0], group_count), 1)
    panel_gain = jnp.sum(
        jnp.where(panel_group[:, None] == group_ids, case_gains[None, :], jnp.float32(0.0)), axis=1
    )
    panel_scale = panel_weight * panel_gain
    weighted = (rows_block.astype(jnp.float32) * panel_scale[None, None, :]).astype(jnp.bfloat16)
    tile_width = weighted.shape[0]
    slab_size = weighted.shape[2]
    left_side = weighted.reshape(tile_width, 6 * slab_size)
    right_side = cols_block.reshape(cols_block.shape[0], 6 * slab_size)
    tile_sign = jnp.where(row_index <= col_index, jnp.float32(1.0), jnp.float32(-1.0))
    half_depth = 3 * slab_size
    partial_tile = pair_products(left_side, right_side, tile_sign, half_depth)
    result = lax.psum_scatter(partial_tile, "panel", scatter_dimension=0, tiled=True)
    return result


def solution(mesh):
    return jax.shard_map(
        local,
        mesh=mesh,
        in_specs=(P(("row", "col"), None, "panel"), P("panel"), P("panel"), P(), P()),
        out_specs=P(("row", "panel"), None, "col"),
        check_vma=False,
    )
```

profile of v0, /device:TPU:4, one launch (start us, length us, event | category | flops | bytes accessed | tf_op | source)
XLA Modules:
  0.0 246.8 jit_solution(13272052365680096868)
XLA Ops:
  6.5 0.7 all-gather.2.cloned.1.call-update
  7.3 0.0 all-reduce.2.cloned.1.call-start
  7.3 57.7 %all-gather.2.cloned.1.call-done = bf16[576,6,512]{2,0,1:T(8,128)(2,1)} async-done(((bf16[72,6,512]{2,0,1:T(8,128)(2,1)}), bf16[576,6,512]{2,0,1:T(8,128)(2,1)}) %all-gather.2.cloned.1.call-update) | async-done | bytes 3538960 | tf_op jit(solution)/shard_map/all_gather | solution.py:31
  65.0 0.2 broadcast_select_fusion
  65.2 3.9 %copy.11 = bf16[576,6,512]{0,2,1:T(8,128)(2,1)} copy(bf16[576,6,512]{2,0,1:T(8,128)(2,1)S(1)} %broadcast_select_fusion) | data formatting | bytes 7077888 | tf_op jit(solution)/shard_map/jit(_where)/select_n | solution.py:8
  69.2 0.0 all-reduce.2.cloned.1.call-update
  69.2 0.0 reduce-scatter.2.cloned.1.call-start
  69.2 0.6 copy-done.2
  69.8 0.7 select_reduce_fusion.1
  70.5 0.6 iota_compare_fusion.3
  71.2 0.1 select_reduce_fusion.2
  71.3 0.1 select_reduce_fusion
  71.4 2.6 %multiply_convert_fusion = bf16[576,6,512]{2,0,1:T(8,128)(2,1)} fusion(bf16[576,6,512]{2,0,1:T(8,128)(2,1)S(1)} %copy-done, f32[512]{0:T(512)S(1)} %mul.21), kind=kLoop, calls=%fused_computation | loop fusion | flops 5308416 | bytes 7079936 | tf_op jit(solution)/shard_map/convert_element_type | solution.py:45
  74.0 5.9 %copy.10 = bf16[576,6,512]{0,2,1:T(8,128)(2,1)} copy(bf16[576,6,512]{2,0,1:T(8,128)(2,1)} %multiply_convert_fusion) | data formatting | bytes 7077888 | tf_op jit(solution)/shard_map/convert_element_type | solution.py:45
  79.9 97.6 %all-reduce.2.cloned.1.call-done = bf16[576,3072]{0,1:T(8,128)(2,1)} async-done(((bf16[576,3072]{0,1:T(8,128)(2,1)}), bf16[576,3072]{0,1:T(8,128)(2,1)}) %all-reduce.2.cloned.1.call-update) | async-done | bytes 3538960 | tf_op jit(solution)/shard_map/psum | solution.py:9
  177.5 3.9 %fusion = f32[576,576]{1,0:T(8,128)S(1)} fusion(bf16[576,3072]{0,1:T(8,128)(2,1)} %all-reduce.2.cloned.1.call-done, bf16[576,3072]{0,1:T(8,128)(2,1)} %bitcast.7), kind=kOutput, calls=%fused_computation.3 | convolution fusion | flops 1019215872 | bytes 5259264 | tf_op jit(solution)/shard_map/dot_general | solution.py:13
  181.4 0.6 copy-done.6
  182.0 1.6 fusion.2
  183.6 1.6 subtract_bitcast_fusion
  185.2 1.6 add_bitcast_fusion
  186.8 1.8 pad_maximum_fusion
  188.6 0.0 reduce-scatter.2.cloned.1.call-update
  188.6 49.7 %reduce-scatter.2.cloned.1.call-done = f32[72,2,576]{2,0,1:T(8,128)} async-done(((f32[576,2,576]{2,0,1:T(8,128)}), f32[72,2,576]{2,0,1:T(8,128)}) %reduce-scatter.2.cloned.1.call-update) | async-done | bytes 331792 | tf_op jit(solution)/shard_map/reduce_scatter | solution.py:53
  238.4 1.9 copy.12
  (15 shorter events, 0.0 us)
Async XLA Ops:
  6.5 58.5 %all-gather.2.cloned.1.call-start = ((), (), s32[]{:S(2)}) async-start(), calls=%async_computation.1 | async-start | bytes 3981312 | tf_op jit(solution)/shard_map/all_gather | solution.py:31
  7.3 170.3 %all-reduce.2.cloned.1.call-start = ((), (), s32[]{:S(2)}) async-start(), calls=%async_computation.2 | async-start | bytes 7864320 | tf_op jit(solution)/shard_map/psum | solution.py:9
  69.1 0.7 copy-start.2
  69.1 2.0 copy-start.4
  69.1 2.2 copy-start.5
  69.1 2.3 copy-start.3
  69.1 2.3 copy-start
  69.2 169.2 %reduce-scatter.2.cloned.1.call-start = ((), (), s32[]{:S(2)}) async-start(), calls=%async_computation.3 | async-start | bytes 3317760 | tf_op jit(solution)/shard_map/reduce_scatter | solution.py:53
  177.5 3.9 %copy-start.1 = (bf16[576,6,512]{0,2,1:T(8,128)(2,1)S(1)}, bf16[576,6,512]{0,2,1:T(8,128)(2,1)}, u32[]{:S(2)}) copy-start(bf16[576,6,512]{0,2,1:T(8,128)(2,1)} %copy.10) | copy-start | bytes 10616836
  177.5 4.5 %copy-start.6 = (bf16[576,3072]{0,1:T(8,128)(2,1)S(1)}, bf16[576,3072]{0,1:T(8,128)(2,1)}, u32[]{:S(2)}) copy-start(bf16[576,3072]{0,1:T(8,128)(2,1)} %all-reduce.2.cloned.1.call-done) | copy-start | bytes 10616836
Sparse Core Ops, SparseCore 0:
  9.5 55.4 all-gather.1
  69.3 108.1 all-reduce.1
  188.7 49.5 reduce-scatter.1
where the time goes:
time: 247 us
  waiting for transfers between devices  206 us (83%)
  between operations  13.2 us (5%)
  local copies, waits for them, and re-layouts  12.9 us (5%)
  matrix products  8.64 us (3%)
  other arithmetic  6.18 us (3%)
    psum x1, waiting for transfers between devices, spread(): return lax.psum(kept, axis)  97.6 us
    all_gather x1, waiting for transfers between devices, local(): rows_block = lax.all_gather(velocity, 'col', axis=0, tiled=True)  57.7 us
    reduce_scatter x1, waiting for transfers between devices, local(): lax.psum_scatter(partial_tile, 'panel', scatter_dimension=0, tiled=True)  49.7 us
    dot_general x4, matrix products, contract(): lax.dot_general(left_side, right_side, (((1,), (1,)), ((), ())), preferre...  8.64 us
    convert_element_type x1, local copies, waits for them, and re-layouts, local(): (rows_block.astype(jnp.float32) * panel_scale[None, None, :]).astype(jnp....  5.93 us
  transfers between devices with their start and end apart: 3, of which 3 were waited for; matrix products, arithmetic and copies ran while one was open for 4% of the time, Pallas kernels for 0%

commit v1 on v0

--- a/solution.py
+++ b/solution.py
@@ -28,7 +28,9 @@
 def local(velocity, panel_weight, panel_group, tile_map, group_gain):
     row_index = lax.axis_index("row")
     col_index = lax.axis_index("col")
-    rows_block = lax.all_gather(velocity, "col", axis=0, tiled=True)
+    rows_block = jnp.concatenate(
+        lax.all_to_all(jnp.stack([velocity] * lax.axis_size("col")), "col", 0, 0), axis=0
+    )
     cols_block = spread(rows_block, "row", col_index)
     chosen = (lax.broadcasted_iota(jnp.int32, tile_map.shape, 0) == row_index) & (
         lax.broadcasted_iota(jnp.int32, tile_map.shape, 1) == col_index

time: 247 us -> 277 us (1.12)
  the two profiles are of different devices: /device:TPU:4 before, /device:TPU:6 now
where the time goes in v1:
time: 277 us
  waiting for transfers between devices  220 us (79%)
  local copies, waits for them, and re-layouts  20 us (7%)
  between operations  13.5 us (5%)
  starting transfers between devices  10.6 us (4%)
  matrix products  7.96 us (3%)
  other arithmetic  4.46 us (2%)
    psum x1, waiting for transfers between devices, spread(): return lax.psum(kept, axis)  88.1 us
    all_to_all x1, waiting for transfers between devices, local(): lax.all_to_all(jnp.stack([velocity] * lax.axis_size('col')), 'col', 0, 0)  82.9 us
    reduce_scatter x1, waiting for transfers between devices, local(): lax.psum_scatter(partial_tile, 'panel', scatter_dimension=0, tiled=True)  49.3 us
    unnamed x14, local copies, waits for them, and re-layouts  11.5 us
    all_to_all x1, starting transfers between devices, local(): lax.all_to_all(jnp.stack([velocity] * lax.axis_size('col')), 'col', 0, 0)  10.3 us
    dot_general x4, matrix products, contract(): lax.dot_general(left_side, right_side, (((1,), (1,)), ((), ())), preferre...  7.96 us
  transfers between devices with their start and end apart: 3, of which 3 were waited for; matrix products, arithmetic and copies ran while one was open for 4% of the time, Pallas kernels for 0%

profile of v1, /device:TPU:6, one launch (start us, length us, event | category | flops | bytes accessed | tf_op | source)
XLA Modules:
  0.0 276.9 jit_solution(4369317214743275230)
XLA Ops:
  6.5 3.1 %stack.8 = bf16[8,72,6,512]{3,1,2,0:T(8,128)(2,1)} broadcast(bf16[72,6,512]{2,0,1:T(8,128)(2,1)} %param.5), dimensions={1,2,3} | broadcast | bytes 3981312 | tf_op jit(solution)/shard_map/stack | solution.py:32
  9.6 10.3 %all-to-all-start = ((bf16[8,72,6,512]{3,1,2,0:T(8,128)(2,1)}), bf16[8,72,6,512]{3,1,2,0:T(8,128)(2,1)S(1)}, u32[]{:S(2)}, u32[]{:S(2)}) async-start(bf16[8,72,6,512]{3,1,2,0:T(8,128)(2,1)} %stack.8), calls=%async_computation | async-start | bytes 7077888 | tf_op jit(solution)/shard_map/all_to_all | solution.py:32
  20.0 82.9 %all-to-all-done = bf16[8,72,6,512]{3,1,2,0:T(8,128)(2,1)S(1)} async-done(((bf16[8,72,6,512]{3,1,2,0:T(8,128)(2,1)}), bf16[8,72,6,512]{3,1,2,0:T(8,128)(2,1)S(1)}, u32[]{:S(2)}, u32[]{:S(2)}) %all-to-all-start) | async-done | bytes 3538976 | tf_op jit(solution)/shard_map/all_to_all | solution.py:32
  102.9 0.2 broadcast_select_fusion
  103.1 1.4 copy.14
  104.6 4.2 %copy.17 = bf16[72,8,6,512]{3,1,2,0:T(8,128)(2,1)} copy(bf16[72,8,6,512]{3,2,1,0:T(8,128)(2,1)S(1)} %bitcast.12) | data formatting | bytes 7077888
  108.8 0.2 reduce-scatter.2.cloned.1.call-start
  109.0 0.4 copy-done.1
  109.4 0.7 select_reduce_fusion.1
  110.1 0.6 iota_compare_fusion.3
  110.8 0.1 select_reduce_fusion.2
  110.9 0.1 select_reduce_fusion
  111.0 0.6 mul.28
  111.6 1.4 copy.13
  113.1 6.9 %copy.16 = f32[72,8,6,512]{3,1,2,0:T(8,128)S(1)} copy(f32[72,8,6,512]{3,2,1,0:T(8,128)S(1)} %bitcast.10) | data formatting | bytes 14155776
  120.0 0.9 multiply_convert_fusion
  120.9 88.1 %all-reduce.2.cloned.1.call-done = bf16[576,3072]{1,0:T(8,128)(2,1)} async-done(((bf16[576,3072]{1,0:T(8,128)(2,1)}), bf16[576,3072]{1,0:T(8,128)(2,1)}) %all-reduce.2.cloned.1.call-update) | async-done | bytes 3538960 | tf_op jit(solution)/shard_map/psum | solution.py:9
  209.0 3.2 %fusion.4 = f32[576,576]{1,0:T(8,128)S(1)} fusion(bf16[576,3072]{1,0:T(8,128)(2,1)S(1)} %multiply_convert_fusion, bf16[576,3072]{1,0:T(8,128)(2,1)} %all-reduce.2.cloned.1.call-done), kind=kOutput, calls=%fused_computation.7 | convolution fusion | flops 1019215872 | bytes 4866048 | tf_op jit(solution)/shard_map/dot_general | solution.py:13
  212.2 1.6 fusion.8
  213.8 1.6 subtract_bitcast_fusion
  215.4 1.6 add_bitcast_fusion
  217.0 1.8 pad_maximum_fusion
  218.8 49.3 %reduce-scatter.2.cloned.1.call-done = f32[72,2,576]{2,0,1:T(8,128)} async-done(((f32[576,2,576]{2,0,1:T(8,128)}), f32[72,2,576]{2,0,1:T(8,128)}) %reduce-scatter.2.cloned.1.call-update) | async-done | bytes 331792 | tf_op jit(solution)/shard_map/reduce_scatter | solution.py:55
  268.1 1.9 copy.15
  (17 shorter events, 0.1 us)
Async XLA Ops:
  9.6 93.3 %all-to-all-start = ((bf16[8,72,6,512]{3,1,2,0:T(8,128)(2,1)}), bf16[8,72,6,512]{3,1,2,0:T(8,128)(2,1)S(1)}, u32[]{:S(2)}, u32[]{:S(2)}) async-start(bf16[8,72,6,512]{3,1,2,0:T(8,128)(2,1)} %stack.8), calls=%async_computation | async-start | bytes 7077888 | tf_op jit(solution)/shard_map/all_to_all | solution.py:32
  19.9 189.1 %all-reduce.2.cloned.1.call-start = ((), (), s32[]{:S(2)}) async-start(), calls=%async_computation.2 | async-start | bytes 7077888 | tf_op jit(solution)/shard_map/psum | solution.py:9
  108.8 0.7 copy-start.1
  108.8 2.0 copy-start.3
  108.8 2.2 copy-start.4
  108.8 2.3 copy-start.2
  108.8 159.3 %reduce-scatter.2.cloned.1.call-start = ((), (), s32[]{:S(2)}) async-start(), calls=%async_computation.3 | async-start | bytes 3317760 | tf_op jit(solution)/shard_map/reduce_scatter | solution.py:55
  113.1 6.9 %copy-start = (f32[3072]{0:T(1024)S(1)}, f32[3072]{0:T(1024)}, u32[]{:S(2)}) copy-start(f32[3072]{0:T(1024)} %mul.28) | copy-start | bytes 36868
  209.0 3.2 %copy-start.5 = (bf16[576,3072]{1,0:T(8,128)(2,1)S(1)}, bf16[576,3072]{1,0:T(8,128)(2,1)}, u32[]{:S(2)}) copy-start(bf16[576,3072]{1,0:T(8,128)(2,1)} %all-reduce.2.cloned.1.call-done) | copy-start | bytes 10616836
Sparse Core Ops, SparseCore 0:
  108.9 100.0 all-reduce.1
  218.9 49.1 reduce-scatter.1

commit v2 on v0

--- a/solution.py
+++ b/solution.py
@@ -6,7 +6,7 @@
 
 def spread(value, axis, source):
     kept = jnp.where(lax.axis_index(axis) == source, value, 0).astype(value.dtype)
-    return lax.psum(kept, axis)
+    return jnp.sum(lax.all_gather(kept, axis), axis=0)
 
 
 def contract(left_side, right_side):

time: 247 us -> 436 us (1.77)
  waiting for transfers between devices: 206 us -> 378 us
  other arithmetic: 6.18 us -> 22.4 us
    all_gather x0 -> x1, waiting for transfers between devices: none -> 270 us  [spread(): return jnp.sum(lax.all_gather(kept, axis), axis=0)]
    psum x1 -> x0, waiting for transfers between devices: 97.6 us -> none  [spread(): return lax.psum(kept, axis)]
    reduce_sum x0 -> x1, other arithmetic: none -> 14.5 us  [spread(): return jnp.sum(lax.all_gather(kept, axis), axis=0)]
  transfers between devices with their start and end apart: 3 -> 3, of which waited for: 3 -> 3; matrix products, arithmetic and copies ran while one was open for 4% -> 2% of each run, Pallas kernels for 0% -> 0%
where the time goes in v2:
time: 436 us
  waiting for transfers between devices  378 us (87%)
  other arithmetic  22.4 us (5%)
  between operations  13.2 us (3%)
  local copies, waits for them, and re-layouts  13 us (3%)
  matrix products  8.64 us (2%)
    all_gather x1, waiting for transfers between devices, spread(): return jnp.sum(lax.all_gather(kept, axis), axis=0)  270 us
    all_gather x1, waiting for transfers between devices, local(): rows_block = lax.all_gather(velocity, 'col', axis=0, tiled=True)  57.7 us
    reduce_scatter x1, waiting for transfers between devices, local(): lax.psum_scatter(partial_tile, 'panel', scatter_dimension=0, tiled=True)  49.6 us
    reduce_sum x1, other arithmetic, spread(): return jnp.sum(lax.all_gather(kept, axis), axis=0)  14.5 us
  transfers between devices with their start and end apart: 3, of which 3 were waited for; matrix products, arithmetic and copies ran while one was open for 2% of the time, Pallas kernels for 0%

profile of v2, /device:TPU:4, one launch (start us, length us, event | category | flops | bytes accessed | tf_op | source)
XLA Modules:
  0.0 435.8 jit_solution(751372124546751644)
XLA Ops:
  6.5 0.7 all-gather.4.cloned.1.call-update
  7.3 0.0 all-gather.6.cloned.1.call-start
  7.3 57.7 %all-gather.4.cloned.1.call-done = bf16[576,6,512]{2,0,1:T(8,128)(2,1)} async-done(((bf16[72,6,512]{2,0,1:T(8,128)(2,1)}), bf16[576,6,512]{2,0,1:T(8,128)(2,1)}) %all-gather.4.cloned.1.call-update) | async-done | bytes 3538960 | tf_op jit(solution)/shard_map/all_gather | solution.py:31
  65.0 2.0 broadcast_select_fusion
  67.0 0.0 all-gather.6.cloned.1.call-update
  67.1 0.0 reduce-scatter.2.cloned.1.call-start
  67.1 0.6 copy-done.3
  67.7 0.7 select_reduce_fusion.1
  68.4 0.6 iota_compare_fusion.3
  69.1 0.1 select_reduce_fusion.2
  69.2 0.1 select_reduce_fusion
  69.3 2.5 multiply_convert_fusion
  71.8 5.9 %copy.12 = bf16[576,6,512]{0,2,1:T(8,128)(2,1)} copy(bf16[576,6,512]{2,0,1:T(8,128)(2,1)} %multiply_convert_fusion) | data formatting | bytes 7077888 | tf_op jit(solution)/shard_map/convert_element_type | solution.py:45
  77.8 270.4 %all-gather.6.cloned.1.call-done = bf16[4608,6,512]{2,0,1:T(8,128)(2,1)} async-done(((bf16[576,6,512]{2,0,1:T(8,128)(2,1)}), bf16[4608,6,512]{2,0,1:T(8,128)(2,1)}) %all-gather.6.cloned.1.call-update) | async-done | bytes 28311568 | tf_op jit(solution)/shard_map/all_gather | solution.py:9
  348.2 14.5 %reduce_sum.42 = bf16[576,6,512]{2,0,1:T(8,128)(2,1)S(1)} reduce(bf16[8,576,6,512]{3,1,0,2:T(8,128)(2,1)} %bitcast.7, bf16[]{:T(256)} %constant.17.clone.1), dimensions={0}, to_apply=%region_3.4 | reduce | flops 12386304 | bytes 31850498 | tf_op jit(solution)/shard_map/reduce_sum | solution.py:9
  362.7 3.9 copy.13
  366.6 3.9 fusion
  370.5 0.6 copy-done.2
  371.1 1.6 fusion.2
  372.7 1.6 subtract_bitcast_fusion
  374.3 1.6 add_bitcast_fusion
  375.9 1.8 pad_maximum_fusion
  377.7 49.6 %reduce-scatter.2.cloned.1.call-done = f32[72,2,576]{2,0,1:T(8,128)} async-done(((f32[576,2,576]{2,0,1:T(8,128)}), f32[72,2,576]{2,0,1:T(8,128)}) %reduce-scatter.2.cloned.1.call-update) | async-done | bytes 331792 | tf_op jit(solution)/shard_map/reduce_scatter | solution.py:53
  427.3 1.9 copy.14
  (16 shorter events, 0.1 us)
Async XLA Ops:
  6.5 58.5 %all-gather.4.cloned.1.call-start = ((), (), s32[]{:S(2)}) async-start(), calls=%async_computation.1 | async-start | bytes 3981312 | tf_op jit(solution)/shard_map/all_gather | solution.py:31
  7.3 340.9 %all-gather.6.cloned.1.call-start = ((), (), s32[]{:S(2)}) async-start(), calls=%async_computation.3 | async-start | bytes 31850496 | tf_op jit(solution)/shard_map/all_gather | solution.py:9
  67.0 0.7 copy-start.3
  67.0 2.0 copy-start.5
  67.0 2.2 copy-start.6
  67.0 2.3 copy-start.4
  67.0 2.3 copy-start
  67.1 360.3 %reduce-scatter.2.cloned.1.call-start = ((), (), s32[]{:S(2)}) async-start(), calls=%async_computation.2 | async-start | bytes 3317760 | tf_op jit(solution)/shard_map/reduce_scatter | solution.py:53
  366.6 3.9 copy-start.1
  366.6 4.5 %copy-start.2 = (bf16[576,6,512]{0,2,1:T(8,128)(2,1)S(1)}, bf16[576,6,512]{0,2,1:T(8,128)(2,1)}, u32[]{:S(2)}) copy-start(bf16[576,6,512]{0,2,1:T(8,128)(2,1)} %copy.13) | copy-start | bytes 10616836
Sparse Core Ops, SparseCore 0:
  9.5 55.4 all-gather.3
  67.2 280.9 all-gather.5
  377.8 49.4 reduce-scatter.1
